TPU v7x, 256 devices: a whole 4x4x8 slice. The times are simulated.
256 devices in a mesh: grp: 8 (over y, core), pan: 32 (over z, x).
Axes of the slice: x: 4, y: 4, z: 8, core: 2. Of those that a mesh axis runs over, the one named last changes fastest.
Arguments:
- anc_rows: bfloat16 [16384, 16384], P('grp', 'pan'), as said below
- row_home: int32 [128], replicated, may hold values from 0 to 127, as said below
- block_lists: int32 [8, 64], replicated, may hold values from 0 to 127, as said below
- front_blocks: int32 [8], replicated, may hold values from 32 to 64, as said below
- panel: bfloat16 [8, 8192, 768], P('grp', 'pan'), may hold values from -0.29882812 to 0.29882812
- pivot_inverse: bfloat16 [8, 768, 768], P('grp'), as said below
Outputs:
- cross_cov: bfloat16 [8, 8192, 768], P('grp', 'pan')
- pivot_cov: float32 [8, 768, 768], P('grp', 'pan')
Inputs may be any that keep to these rules, and one draw needn't show every extreme that they name: `row_home`: A permutation of 0 to 127; the 4 index blocks of each window [4 q, 4 q + 4) have their storage row blocks in one front group. `block_lists`: rising along each row; entries 2 * q to 2 * q + 1 lie in [4 * q, 4 * q + 4). `front_blocks`: some front has all 64 blocks. `anc_rows`: storage row block row_home[b] holds row block b of a symmetric matrix. `pivot_inverse`: lower triangular.
All inputs are finite; a program needn't handle non-finite values.
Results may differ from a plain program's by a relative error of at most 0.0095.
Values may be sent and summed in bfloat16 or wider, within the bound.
A program may use at most 128 MiB of HBM per device.

v0:
```python
import jax
import jax.numpy as jnp
from jax import lax
from jax.sharding import PartitionSpec as P

BLK = 128
P_SIZE = 768


def per_device(anc_rows, row_home, block_lists, front_blocks, panel, pivot_inverse):
    groups = lax.axis_size("grp")
    pan_count = lax.axis_size("pan")
    group_idx = lax.axis_index("grp")
    pan_idx = lax.axis_index("pan")
    block_count = row_home.shape[0]
    front_len = block_lists.shape[1]
    rb_local = front_len // pan_count
    cb_local = anc_rows.shape[1] // BLK
    stored_blocks = anc_rows.shape[0] // BLK
    windows = block_count // cb_local
    win_per_group = windows // groups
    per_src = win_per_group * rb_local
    contract = (((0,), (0,)), ((), ()))
    home_of_window = row_home[cb_local * jnp.arange(windows, dtype=jnp.int32)] // stored_blocks
    win = jnp.argsort(home_of_window * windows + jnp.arange(windows, dtype=jnp.int32))
    win = win.reshape(groups, win_per_group).astype(jnp.int32)
    pos = (rb_local * win[:, :, None] + jnp.arange(rb_local, dtype=jnp.int32)).reshape(
        groups, per_src
    )
    my_pos = lax.dynamic_index_in_dim(pos, group_idx, 0, keepdims=False)
    row_blocks = jnp.take(block_lists, my_pos, axis=1)
    slots = jnp.take(row_home, row_blocks) - stored_blocks * group_idx
    cols = (
        lax.dynamic_slice_in_dim(block_lists, rb_local * pan_idx, rb_local, axis=1)
        - cb_local * pan_idx
    )
    local = anc_rows.reshape(stored_blocks, BLK, cb_local, BLK)
    outgoing = local[slots[:, :, None], :, cols[:, None, :], :]
    received = lax.all_to_all(outgoing, "grp", split_axis=0, concat_axis=0, tiled=True)
    order = jnp.argsort(pos.reshape(groups * per_src)).astype(jnp.int32)
    sigma = jnp.take(received.reshape(groups * per_src, rb_local, BLK, BLK), order, axis=0)
    my_blocks = pan_idx * rb_local + jnp.arange(rb_local, dtype=jnp.int32)
    front_live = lax.dynamic_index_in_dim(front_blocks, group_idx, 0, keepdims=False)
    alive_rows = jnp.repeat(my_blocks < front_live, BLK)
    inverse_pivot = pivot_inverse[0]
    scaled = jnp.dot(panel[0], inverse_pivot, preferred_element_type=jnp.float32)
    scaled = jnp.where(alive_rows[:, None], scaled, jnp.zeros_like(scaled)).astype(jnp.bfloat16)
    full = lax.all_gather(scaled, "pan", axis=0, tiled=True)
    product = lax.dot_general(
        sigma,
        full.reshape(front_len, BLK, P_SIZE),
        (((0, 2), (0, 1)), ((), ())),
        preferred_element_type=jnp.float32,
    ).reshape(rb_local * BLK, P_SIZE)
    cross = jnp.where(alive_rows[:, None], -product, jnp.zeros_like(product)).astype(jnp.bfloat16)
    pivot_rows = P_SIZE // pan_count
    shared = lax.psum_scatter(
        (-lax.dot_general(scaled, cross, contract, preferred_element_type=jnp.float32)).astype(
            jnp.bfloat16
        ),
        "pan",
        scatter_dimension=0,
        tiled=True,
    ).astype(jnp.float32)
    own_columns = lax.dynamic_slice_in_dim(inverse_pivot, pan_idx * pivot_rows, pivot_rows, 1)
    triangle = lax.dot_general(
        own_columns, inverse_pivot, contract, preferred_element_type=jnp.float32
    )
    pivot = triangle + shared
    return (cross[None], pivot[None])


def solution(mesh):
    placed = (P("grp", "pan"), P(), P(), P(), P("grp", "pan", None), P("grp", None, None))
    return jax.shard_map(
        per_device,
        mesh=mesh,
        in_specs=placed,
        out_specs=(P("grp", "pan", None), P("grp", "pan", None)),
        check_vma=False,
    )
```

profile of v0, /device:TPU:8, one launch (start us, length us, event | category | flops | bytes accessed | tf_op | source)
XLA Modules:
  0.0 352.9 jit_solution(3056510419691765363)
XLA Ops:
  7.2 0.0 copy-start
  7.2 0.0 copy-start.1
  7.2 0.0 copy-start.4
  7.2 0.0 copy-start.2
  7.2 0.0 all-gather.2.cloned.1.call-start
  7.3 1.4 dynamic_slice.16
  8.7 0.7 add_compare_fusion
  9.3 0.1 broadcast_bitcast_fusion
  9.4 0.0 copy-done
  9.4 2.2 fusion.3
  11.6 0.0 all-gather.2.cloned.1.call-update
  11.7 1.4 gather_fusion
  13.1 1.6 sort.34
  14.7 0.1 mul.53
  14.7 0.1 copy.20
  14.8 0.1 add.144
  14.9 0.1 broadcast_add_fusion
  15.0 0.2 dynamic-slice_reduce_fusion
  15.2 0.8 copy.23
  16.0 0.6 gather_fusion.1
  16.5 0.1 copy.24
  16.6 0.1 reshape.182
  16.7 0.0 copy-done.1
  16.7 0.8 gather_fusion.2
  17.5 0.1 reshape.181
  17.6 0.1 copy.25
  17.6 0.1 fusion.17
  17.7 0.1 copy.26
  17.8 0.0 copy-done.4
  17.8 0.1 fusion.19
  17.9 0.1 broadcast_or_fusion
  18.0 0.1 reshape.188
  18.1 0.0 copy-done.2
  18.1 2.1 reshape.205
  20.2 2.1 copy.27
  22.4 3.1 gather_fusion.3
  25.4 6.6 %all-to-all-start = ((bf16[8,8,2,128,128]{4,3,2,1,0:T(8,128)(2,1)}), bf16[8,8,2,128,128]{4,3,2,1,0:T(8,128)(2,1)}, u32[]{:S(2)}, u32[]{:S(2)}) async-start(bf16[8,8,2,128,128]{4,3,2,1,0:T(8,128)(2,1)} %bitcast.59), calls=%async_computation | async-start | bytes 8388608 | tf_op jit(solution)/shard_map/all_to_all | solution.py:39
  32.1 0.0 reduce-scatter.2.cloned.1.call-start
  32.1 0.1 copy.21
  32.2 0.1 add.139
  32.3 2.0 sort.35
  34.4 46.0 %all-to-all-done = bf16[8,8,2,128,128]{4,3,2,1,0:T(8,128)(2,1)} async-done(((bf16[8,8,2,128,128]{4,3,2,1,0:T(8,128)(2,1)}), bf16[8,8,2,128,128]{4,3,2,1,0:T(8,128)(2,1)}, u32[]{:S(2)}, u32[]{:S(2)}) %all-to-all-start) | async-done | bytes 4194336 | tf_op jit(solution)/shard_map/all_to_all | solution.py:39
  80.4 5.2 %gather_fusion.4 = bf16[64,2,128,128]{3,2,1,0:T(8,128)(2,1)} fusion(bf16[64,2,128,128]{3,2,1,0:T(8,128)(2,1)} %bitcast.8, s32[1024]{0:T(1024)S(1)} %pad_clamp_fusion), kind=kCustom, calls=%fused_computation.4 | custom fusion | bytes 8388864 | tf_op jit(solution)/shard_map/jit(_take)/gather | solution.py:41
  85.7 4.5 %select_bitcast_fusion = bf16[2,128,64,128]{1,3,0,2:T(8,128)(2,1)} fusion(bf16[64,2,128,128]{3,2,1,0:T(8,128)(2,1)} %gather_fusion.4, pred[64]{0:T(512)(128)(4,1)S(1)} %compare_and_fusion.1), kind=kLoop, calls=%fused_computation.5 | loop fusion | flops 2097152 | bytes 8388672 | tf_op jit(solution)/shard_map/jit(_take)/select_n | solution.py:41
  90.2 6.4 %copy.32 = bf16[2,128,64,128]{3,1,0,2:T(8,128)(2,1)} copy(bf16[2,128,64,128]{1,3,0,2:T(8,128)(2,1)} %select_bitcast_fusion) | data formatting | bytes 8388608 | tf_op jit(solution)/shard_map/dot_general | solution.py:49
  96.6 37.7 %all-gather.2.cloned.1.call-done = bf16[8192,768]{1,0:T(8,128)(2,1)} async-done(((bf16[256,768]{1,0:T(8,128)(2,1)}), bf16[8192,768]{1,0:T(8,128)(2,1)}) %all-gather.2.cloned.1.call-update) | async-done | bytes 12582928 | tf_op jit(solution)/shard_map/all_gather | solution.py:48
  134.3 0.0 copy-start.3
  134.3 8.8 %fusion.2 = bf16[256,768]{1,0:T(8,128)(2,1)S(1)} fusion(bf16[256,64,128]{2,0,1:T(8,128)(2,1)} %bitcast.60, bf16[64,128,768]{2,1,0:T(8,128)(2,1)} %bitcast.63, pred[256]{0:T(512)(128)(4,1)S(1)} %broadcast_bitcast_fusion), kind=kOutput, calls=%fused_computation.11 | convolution fusion | flops 3221815296 | bytes 17170688 | tf_op jit(solution)/shard_map/dot_general | solution.py:49
  143.1 0.0 copy-done.3
  143.1 0.0 copy-start.5
  143.1 1.5 negate_convert_fusion
  144.7 0.0 reduce-scatter.2.cloned.1.call-update
  144.7 199.6 %reduce-scatter.2.cloned.1.call-done = bf16[24,768]{1,0:T(8,128)(2,1)} async-done(((bf16[768,768]{1,0:T(8,128)(2,1)}), bf16[24,768]{1,0:T(8,128)(2,1)}) %reduce-scatter.2.cloned.1.call-update) | async-done | bytes 36880 | tf_op jit(solution)/shard_map/reduce_scatter | solution.py:57
  344.3 1.8 fusion.10
  346.1 0.0 copy-done.5
  (17 shorter events, 0.1 us)
Async XLA Ops:
  7.2 2.2 copy-start
  7.2 9.5 %copy-start.1 = (s32[128]{0:T(128)S(1)}, s32[128]{0:T(128)}, u32[]{:S(2)}) copy-start(s32[128]{0:T(128)} %param.7) | copy-start | bytes 1540
  7.2 10.6 %copy-start.4 = (s32[8,64]{1,0:T(8,128)S(1)}, s32[8,64]{1,0:T(8,128)}, u32[]{:S(2)}) copy-start(s32[8,64]{1,0:T(8,128)} %param.8) | copy-start | bytes 6148
  7.2 10.9 %copy-start.2 = (bf16[2048,512]{1,0:T(8,128)(2,1)S(1)}, bf16[2048,512]{1,0:T(8,128)(2,1)}, u32[]{:S(2)}) copy-start(bf16[2048,512]{1,0:T(8,128)(2,1)} %param.6) | copy-start | bytes 6291460
  7.2 127.1 %all-gather.2.cloned.1.call-start = ((), (), s32[]{:S(2)}) async-start(), calls=%async_computation.2 | async-start | bytes 12976128 | tf_op jit(solution)/shard_map/all_gather | solution.py:48
  25.4 55.0 %all-to-all-start = ((bf16[8,8,2,128,128]{4,3,2,1,0:T(8,128)(2,1)}), bf16[8,8,2,128,128]{4,3,2,1,0:T(8,128)(2,1)}, u32[]{:S(2)}, u32[]{:S(2)}) async-start(bf16[8,8,2,128,128]{4,3,2,1,0:T(8,128)(2,1)} %bitcast.59), calls=%async_computation | async-start | bytes 8388608 | tf_op jit(solution)/shard_map/all_to_all | solution.py:39
  32.1 312.2 %reduce-scatter.2.cloned.1.call-start = ((), (), s32[]{:S(2)}) async-start(), calls=%async_computation.3 | async-start | bytes 1216512 | tf_op jit(solution)/shard_map/reduce_scatter | solution.py:57
  134.3 8.8 %copy-start.3 = (bf16[256,768]{1,0:T(8,128)(2,1)S(1)}, bf16[256,768]{1,0:T(8,128)(2,1)}, u32[]{:S(2)}) copy-start(bf16[256,768]{1,0:T(8,128)(2,1)} %fusion.3) | copy-start | bytes 1179652
  143.1 203.0 %copy-start.5 = (bf16[256,768]{1,0:T(8,128)(2,1)}, bf16[256,768]{1,0:T(8,128)(2,1)S(1)}, u32[]{:S(2)}) copy-start(bf16[256,768]{1,0:T(8,128)(2,1)S(1)} %fusion.2) | copy-start | bytes 1179652
Sparse Core Ops, SparseCore 0:
  11.8 122.4 all-gather.1
  144.8 199.4 reduce-scatter.1
where the time goes:
time: 353 us
  waiting for transfers between devices  283 us (80%)
  local copies, waits for them, and re-layouts  25.1 us (7%)
  matrix products  14.3 us (4%)
  between operations  14.2 us (4%)
  other arithmetic  9.24 us (3%)
  starting transfers between devices  6.68 us (2%)
    reduce_scatter x1, waiting for transfers between devices, per_device(): lax.psum_scatter((-lax.dot_general(scaled, cross, contract, preferred_ele...  200 us
    all_to_all x1, waiting for transfers between devices, per_device(): lax.all_to_all(outgoing, 'grp', split_axis=0, concat_axis=0, tiled=True)  46 us
    all_gather x1, waiting for transfers between devices, per_device(): full = lax.all_gather(scaled, 'pan', axis=0, tiled=True)  37.7 us
    dot_general x1, matrix products, per_device(): lax.dot_general(sigma, full.reshape(front_len, BLK, P_SIZE), (((0, 2), (0...  8.79 us
  transfers between devices with their start and end apart: 3, of which 3 were waited for; matrix products, arithmetic and copies ran while one was open for 9% of the time, Pallas kernels for 0%

commit v1 on v0

--- a/solution.py
+++ b/solution.py
@@ -45,7 +45,10 @@
     inverse_pivot = pivot_inverse[0]
     scaled = jnp.dot(panel[0], inverse_pivot, preferred_element_type=jnp.float32)
     scaled = jnp.where(alive_rows[:, None], scaled, jnp.zeros_like(scaled)).astype(jnp.bfloat16)
-    full = lax.all_gather(scaled, "pan", axis=0, tiled=True)
+    form_widths_by_axis = lambda z, axis_id: jnp.concatenate(
+        lax.all_to_all(jnp.stack([z for _ in range(lax.axis_size(axis_id))]), axis_id, 0, 0), 0
+    )
+    full = form_widths_by_axis(scaled, "pan")
     product = lax.dot_general(
         sigma,
         full.reshape(front_len, BLK, P_SIZE),

time: 353 us -> 616 us (1.75)
  waiting for transfers between devices: 283 us -> 532 us
  starting transfers between devices: 6.68 us -> 16.5 us
    all_to_all x0 -> x1, waiting for transfers between devices: none -> 265 us  [per_device(): lax.all_to_all(jnp.stack([z for _ in range(lax.axis_size(axis_id))]), axi...]
    all_gather x1 -> x0, waiting for transfers between devices: 37.7 us -> none  [per_device(): full = lax.all_gather(scaled, 'pan', axis=0, tiled=True)]
    reduce_scatter x1, waiting for transfers between devices: 200 us -> 220 us  [per_device(): lax.psum_scatter((-lax.dot_general(scaled, cross, contract, preferred_ele...]
    all_to_all x0 -> x1, starting transfers between devices: none -> 9.69 us  [per_device(): lax.all_to_all(jnp.stack([z for _ in range(lax.axis_size(axis_id))]), axi...]
  transfers between devices with their start and end apart: 3 -> 3, of which waited for: 3 -> 3; matrix products, arithmetic and copies ran while one was open for 9% -> 3% of each run, Pallas kernels for 0% -> 0%
where the time goes in v1:
time: 616 us; the launch traced here: 615 us
  waiting for transfers between devices  532 us (86%)
  local copies, waits for them, and re-layouts  30.9 us (5%)
  starting transfers between devices  16.5 us (3%)
  between operations  14.2 us (2%)
  matrix products  12.7 us (2%)
  other arithmetic  9.26 us (2%)
    all_to_all x1, waiting for transfers between devices, per_device(): lax.all_to_all(jnp.stack([z for _ in range(lax.axis_size(axis_id))]), axi...  265 us
    reduce_scatter x1, waiting for transfers between devices, per_device(): lax.psum_scatter((-lax.dot_general(scaled, cross, contract, preferred_ele...  220 us
    all_to_all x1, waiting for transfers between devices, per_device(): lax.all_to_all(outgoing, 'grp', split_axis=0, concat_axis=0, tiled=True)  46.5 us
  transfers between devices with their start and end apart: 3, of which 3 were waited for; matrix products, arithmetic and copies ran while one was open for 3% of the time, Pallas kernels for 0%

profile of v1, /device:TPU:8, one launch (start us, length us, event | category | flops | bytes accessed | tf_op | source)
XLA Modules:
  0.0 615.4 jit_solution(1720224530766737796)
XLA Ops:
  7.2 0.0 copy-start
  7.2 0.0 copy-start.2
  7.2 0.0 copy-start.1
  7.2 0.1 add.144
  7.3 1.5 gather_fusion
  8.9 1.6 sort.34
  10.5 0.1 mul.53
  10.6 0.1 copy.20
  10.7 0.1 broadcast_add_fusion
  10.7 0.2 dynamic-slice_reduce_fusion
  11.0 0.8 copy.23
  11.7 0.6 gather_fusion.1
  12.3 0.1 copy.24
  12.4 0.1 reshape.180
  12.5 1.4 gather_fusion.2
  13.9 0.1 reshape.179
  14.0 0.1 copy.25
  14.0 0.1 fusion.17
  14.1 0.1 copy.26
  14.2 0.0 copy-done.2
  14.2 0.1 fusion.19
  14.3 0.1 broadcast_or_fusion
  14.4 0.1 reshape.186
  14.5 0.0 copy-done.1
  14.5 2.1 reshape.203
  16.6 2.1 copy.27
  18.8 3.1 gather_fusion.3
  21.8 0.0 copy-start.4
  21.8 0.0 copy-start.3
  21.8 6.8 %all-to-all-start = ((bf16[8,8,2,128,128]{4,3,2,1,0:T(8,128)(2,1)}), bf16[8,8,2,128,128]{4,3,2,1,0:T(8,128)(2,1)}, u32[]{:S(2)}, u32[]{:S(2)}) async-start(bf16[8,8,2,128,128]{4,3,2,1,0:T(8,128)(2,1)} %bitcast.59), calls=%async_computation | async-start | bytes 8388608 | tf_op jit(solution)/shard_map/all_to_all | solution.py:39
  28.6 0.0 copy-done.4
  28.6 0.6 dynamic_slice.16
  29.2 0.7 add_compare_fusion
  29.9 0.1 broadcast_bitcast_fusion
  29.9 0.0 copy-done
  29.9 0.0 copy-done.3
  29.9 0.5 fusion.3
  30.4 46.5 %all-to-all-done = bf16[8,8,2,128,128]{4,3,2,1,0:T(8,128)(2,1)} async-done(((bf16[8,8,2,128,128]{4,3,2,1,0:T(8,128)(2,1)}), bf16[8,8,2,128,128]{4,3,2,1,0:T(8,128)(2,1)}, u32[]{:S(2)}, u32[]{:S(2)}) %all-to-all-start) | async-done | bytes 4194336 | tf_op jit(solution)/shard_map/all_to_all | solution.py:39
  77.0 5.9 stack.2
  82.9 9.7 %all-to-all-start.1 = ((bf16[32,256,768]{2,1,0:T(8,128)(2,1)}), bf16[32,256,768]{2,1,0:T(8,128)(2,1)}, u32[]{:S(2)}, u32[]{:S(2)}) async-start(bf16[32,256,768]{2,1,0:T(8,128)(2,1)} %stack.2), calls=%async_computation.1 | async-start | bytes 25165824 | tf_op jit(solution)/shard_map/all_to_all | solution.py:49
  92.6 0.0 reduce-scatter.2.cloned.1.call-start
  92.6 0.1 copy.21
  92.7 0.1 add.139
  92.8 2.0 sort.35
  94.9 5.2 gather_fusion.4
  100.1 4.6 select_bitcast_fusion
  104.7 6.3 %copy.32 = bf16[2,128,64,128]{3,1,0,2:T(8,128)(2,1)} copy(bf16[2,128,64,128]{1,3,0,2:T(8,128)(2,1)} %select_bitcast_fusion) | data formatting | bytes 8388608 | tf_op jit(solution)/shard_map/dot_general | solution.py:52
  111.1 264.8 %all-to-all-done.1 = bf16[32,256,768]{2,1,0:T(8,128)(2,1)} async-done(((bf16[32,256,768]{2,1,0:T(8,128)(2,1)}), bf16[32,256,768]{2,1,0:T(8,128)(2,1)}, u32[]{:S(2)}, u32[]{:S(2)}) %all-to-all-start.1) | async-done | bytes 12582944 | tf_op jit(solution)/shard_map/all_to_all | solution.py:49
  375.9 8.9 %fusion.2 = bf16[256,768]{1,0:T(8,128)(2,1)S(1)} fusion(bf16[256,64,128]{2,0,1:T(8,128)(2,1)} %bitcast.60, bf16[64,128,768]{2,1,0:T(8,128)(2,1)} %bitcast.14, pred[256]{0:T(512)(128)(4,1)S(1)} %broadcast_bitcast_fusion), kind=kOutput, calls=%fused_computation.11 | convolution fusion | flops 3221815296 | bytes 17170688 | tf_op jit(solution)/shard_map/dot_general | solution.py:52
  384.8 0.0 copy-start.5
  384.8 1.5 negate_convert_fusion
  386.3 0.0 reduce-scatter.2.cloned.1.call-update
  386.4 220.4 %reduce-scatter.2.cloned.1.call-done = bf16[24,768]{1,0:T(8,128)(2,1)} async-done(((bf16[768,768]{1,0:T(8,128)(2,1)}), bf16[24,768]{1,0:T(8,128)(2,1)}) %reduce-scatter.2.cloned.1.call-update) | async-done | bytes 36880 | tf_op jit(solution)/shard_map/reduce_scatter | solution.py:60
  606.8 1.8 fusion.10
  608.6 0.0 copy-done.5
  (17 shorter events, 0.1 us)
Async XLA Ops:
  7.2 22.8 %copy-start = (bf16[1,768,768]{2,1,0:T(8,128)(2,1)S(1)}, bf16[1,768,768]{2,1,0:T(8,128)(2,1)}, u32[]{:S(2)}) copy-start(bf16[1,768,768]{2,1,0:T(8,128)(2,1)} %param.11) | copy-start | bytes 3538948
  7.2 7.0 %copy-start.2 = (s32[8,64]{1,0:T(8,128)S(1)}, s32[8,64]{1,0:T(8,128)}, u32[]{:S(2)}) copy-start(s32[8,64]{1,0:T(8,128)} %param.8) | copy-start | bytes 6148
  7.2 7.3 %copy-start.1 = (bf16[2048,512]{1,0:T(8,128)(2,1)S(1)}, bf16[2048,512]{1,0:T(8,128)(2,1)}, u32[]{:S(2)}) copy-start(bf16[2048,512]{1,0:T(8,128)(2,1)} %param.6) | copy-start | bytes 6291460
  21.8 6.8 %copy-start.4 = (s32[8]{0:T(128)S(1)}, s32[8]{0:T(128)}, u32[]{:S(2)}) copy-start(s32[8]{0:T(128)} %param.9) | copy-start | bytes 100
  21.8 8.1 %copy-start.3 = (bf16[1,256,768]{2,1,0:T(8,128)(2,1)S(1)}, bf16[1,256,768]{2,1,0:T(8,128)(2,1)}, u32[]{:S(2)}) copy-start(bf16[1,256,768]{2,1,0:T(8,128)(2,1)} %param.10) | copy-start | bytes 1179652
  21.8 55.1 %all-to-all-start = ((bf16[8,8,2,128,128]{4,3,2,1,0:T(8,128)(2,1)}), bf16[8,8,2,128,128]{4,3,2,1,0:T(8,128)(2,1)}, u32[]{:S(2)}, u32[]{:S(2)}) async-start(bf16[8,8,2,128,128]{4,3,2,1,0:T(8,128)(2,1)} %bitcast.59), calls=%async_computation | async-start | bytes 8388608 | tf_op jit(solution)/shard_map/all_to_all | solution.py:39
  82.9 293.0 %all-to-all-start.1 = ((bf16[32,256,768]{2,1,0:T(8,128)(2,1)}), bf16[32,256,768]{2,1,0:T(8,128)(2,1)}, u32[]{:S(2)}, u32[]{:S(2)}) async-start(bf16[32,256,768]{2,1,0:T(8,128)(2,1)} %stack.2), calls=%async_computation.1 | async-start | bytes 25165824 | tf_op jit(solution)/shard_map/all_to_all | solution.py:49
  92.6 514.2 %reduce-scatter.2.cloned.1.call-start = ((), (), s32[]{:S(2)}) async-start(), calls=%async_computation.3 | async-start | bytes 1216512 | tf_op jit(solution)/shard_map/reduce_scatter | solution.py:60
  384.8 223.8 %copy-start.5 = (bf16[256,768]{1,0:T(8,128)(2,1)}, bf16[256,768]{1,0:T(8,128)(2,1)S(1)}, u32[]{:S(2)}) copy-start(bf16[256,768]{1,0:T(8,128)(2,1)S(1)} %fusion.2) | copy-start | bytes 1179652
Sparse Core Ops, SparseCore 0:
  386.5 220.2 reduce-scatter.1
